TPU v7x, 512 devices: a whole 4x8x8 slice. The times are simulated.
512 devices in a mesh: pb: 16 (over x, y_lo), ka: 32 (over y_hi, z, core).
Axes of the slice: x: 4, y: 8 (y_hi: 2, y_lo: 4; y = y_hi * 4 + y_lo), z: 8, core: 2. Of those that a mesh axis runs over, the one named last changes fastest.
Arguments:
- tokens: bfloat16 [8192, 7168], P('ka', 'pb'), may hold values from -6 to 6
- kv_weight: bfloat16 [7168, 576], P('pb'), may hold values from -0.0625 to 0.0625
- queries: bfloat16 [8192, 36864], P('pb', 'ka'), may hold values from -384 to 384
- block_list: int32 [64, 16], P('pb'), may hold values from -1 to 63, as said below
Outputs:
- attended: bfloat16 [8192, 32768], P('pb', 'ka')
Inputs may be any that keep to these rules, and one draw needn't show every extreme that they name: `block_list`: row i lists distinct key blocks j <= i in ascending order, followed by -1 in its unused slots; every row lists block 0; the row of the last block fills all 16 slots. The rows of one aligned group of 4 query blocks list at most 1 distinct blocks of one aligned group of 2 key blocks, and 1 is reached in every draw.
All inputs are finite; a program needn't handle non-finite values.
Results may differ from a plain program's by a relative error of at most 0.012.
Values may be sent and summed in bfloat16 or wider, within the bound.
A program may use at most 64 MiB of HBM per device.

v0:
```python
import math

import jax
import jax.numpy as jnp
from jax import lax
from jax.sharding import Mesh
from jax.sharding import PartitionSpec as P

KVL = 512
RD = 64
QK = 192
BLK = 128
MAXSEL = 16
KA = ("ka_0", "ka_1", "ka_2")


def cut_along(x, dim, devices):
    before, after = (x.shape[:dim], x.shape[dim + 1 :])
    return jnp.moveaxis(x.reshape(*before, devices, -1, *after), dim, 0)


def sum_at_owner(x, axis, dim):
    pieces = cut_along(x, dim, lax.axis_size(axis))
    arrived = lax.all_to_all(pieces, axis, split_axis=0, concat_axis=0, tiled=True)
    return arrived.sum(axis=0)


def filled_up(lines, devices):
    spare = -len(lines) % devices
    return jnp.pad(lines, [(0, spare)] + [(0, 0)] * (lines.ndim - 1))


def joined_along(pieces, dim):
    pieces = jnp.moveaxis(pieces, 0, dim)
    dims = pieces.shape
    return pieces.reshape(*dims[:dim], dims[dim] * dims[dim + 1], *dims[dim + 2 :])


def from_everyone(x, axis):
    devices = lax.axis_size(axis)
    return lax.all_to_all(jnp.broadcast_to(x[None], (devices, *x.shape)), axis, 0, 0, tiled=True)


def gathered_copies(x, axis, dim):
    return joined_along(from_everyone(x, axis), dim)


def nested_sum(x, axes):
    lines = x.reshape(-1, x.shape[-1])
    own = sum_at_owner(filled_up(lines, lax.axis_size(axes)), axes, 0)
    whole = gathered_copies(own, axes, 0)
    return whole[: len(lines)].reshape(x.shape)


def gather_in_order(x, axes, turns):
    pieces = x[None]
    for k in turns:
        pieces = lax.all_gather(pieces, axes[k], axis=0, tiled=True)
    current = [lax.axis_size(axes[k]) for k in reversed(turns)]
    pieces = pieces.reshape(*current, *x.shape)
    turned = sorted(range(len(turns)), key=lambda place: turns[len(turns) - 1 - place])
    return pieces.transpose(*turned, *range(len(turns), pieces.ndim)).reshape(-1, *x.shape)


def whole_of(x, axes, turns, dim):
    return joined_along(gather_in_order(x, axes, turns), dim)


def scale_rows(matrix):
    return matrix * lax.rsqrt(jnp.mean(matrix * matrix, axis=-1, keepdims=True) + 1e-06)


def rotate_cols(rotary, positions):
    half = rotary.shape[1] // 2
    steps = jnp.arange(half, dtype=jnp.float32)
    freq = jnp.exp(steps * (-2.0 * math.log(10000.0) / rotary.shape[1]))
    angle = positions.astype(jnp.float32)[:, None] * freq[None, :]
    cosine = jnp.cos(angle)
    sine = jnp.sin(angle)
    first = rotary[:, :half]
    second = rotary[:, half:]
    return jnp.concatenate([first * cosine - second * sine, second * cosine + first * sine], axis=1)


def per_device(tokens, kv_weight, queries, block_list):
    width = KVL + RD
    stripe_count = lax.axis_size(KA)
    slot_cap = max(1, MAXSEL // stripe_count)
    partial_value = jnp.dot(tokens, kv_weight, preferred_element_type=jnp.float32)
    summed_scores = nested_sum(partial_value, "pb")
    local_count = summed_scores.shape[0]
    row_pos = lax.axis_index(KA) * local_count + jnp.arange(local_count, dtype=jnp.int32)
    latent = scale_rows(summed_scores[:, :KVL])
    rotary = rotate_cols(summed_scores[:, KVL:], row_pos)
    local_pairs = jnp.concatenate([latent, rotary], axis=1).astype(jnp.bfloat16)
    run_blocks = local_count // BLK
    total_blocks = run_blocks * stripe_count
    chosen = jnp.maximum(block_list, 0)
    block_ids = jnp.arange(total_blocks, dtype=jnp.int32)
    listed_any = jnp.any(block_list[:, :, None] == block_ids[None, None, :], axis=(0, 1))
    listed_runs = listed_any.reshape(stripe_count, run_blocks).astype(jnp.int32)
    run_rank = jnp.cumsum(listed_runs, axis=1) - 1
    own_run = lax.axis_index(KA)
    own_listed = lax.dynamic_index_in_dim(listed_runs, own_run, 0, keepdims=False)
    own_rank = lax.dynamic_index_in_dim(run_rank, own_run, 0, keepdims=False)
    slot_ids = jnp.arange(slot_cap, dtype=jnp.int32)
    placed = (own_listed[None, :] == 1) & (own_rank[None, :] == slot_ids[:, None])
    local_pick = jnp.sum(
        jnp.where(placed, jnp.arange(run_blocks, dtype=jnp.int32)[None, :], 0), axis=1
    )
    packed = local_pairs.reshape(run_blocks, BLK, width)[local_pick].reshape(slot_cap * BLK, width)
    key_pool = whole_of(packed, KA, (0, 1, 2), 0)
    slot_table = block_ids // run_blocks * slot_cap + run_rank.reshape(total_blocks)
    pool_index = jnp.sum(
        jnp.where(chosen[:, :, None] == block_ids[None, None, :], slot_table[None, None, :], 0),
        axis=2,
    )
    pool_blocks = key_pool.reshape(-1, BLK, width)
    query_rows = queries.shape[0]
    query_count = query_rows // BLK
    head_count = queries.shape[1] // width
    first_block = lax.axis_index("pb") * query_count
    offsets = jnp.arange(BLK, dtype=jnp.int32)
    factor = 1.0 / math.sqrt(QK)
    grouped = queries.reshape(query_count // 2, 2, BLK, head_count, width)

    def attend(inputs):
        group, query_couple, index_pair, listed_pair, chosen_pair = inputs
        selected_keys = pool_blocks[index_pair].reshape(2, MAXSEL * BLK, width)
        selected_values = selected_keys[:, :, :KVL]
        scores = (
            jnp.einsum(
                "wfer,wur->wefu", query_couple, selected_keys, preferred_element_type=jnp.float32
            )
            * factor
        )
        query_pos = (first_block + group * 2 + jnp.arange(2, dtype=jnp.int32))[
            :, None
        ] * BLK + offsets[None, :]
        key_pos = (chosen_pair[:, :, None] * BLK + offsets[None, None, :]).reshape(2, MAXSEL * BLK)
        slot_live = jnp.broadcast_to((listed_pair >= 0)[:, :, None], (2, MAXSEL, BLK)).reshape(
            2, MAXSEL * BLK
        )
        permitted_mask = slot_live[:, None, :] & (key_pos[:, None, :] <= query_pos[:, :, None])
        scores = jnp.where(permitted_mask[:, None], scores, -jnp.inf)
        highest = jnp.max(scores, axis=-1, keepdims=True)
        weights = jnp.exp(scores - highest)
        weight_brain_float = (weights / jnp.sum(weights, axis=-1, keepdims=True)).astype(
            jnp.bfloat16
        )
        blended = jnp.einsum(
            "stvl,slz->svtz",
            weight_brain_float,
            selected_values,
            preferred_element_type=jnp.float32,
        )
        return blended.astype(jnp.bfloat16).reshape(2 * BLK, head_count * KVL)

    outputs = lax.map(
        attend,
        (
            jnp.arange(query_count // 2, dtype=jnp.int32),
            grouped,
            pool_index.reshape(query_count // 2, 2, MAXSEL),
            block_list.reshape(query_count // 2, 2, MAXSEL),
            chosen.reshape(query_count // 2, 2, MAXSEL),
        ),
    )
    return outputs.reshape(query_rows, head_count * KVL)


def solution(mesh):
    split = Mesh(mesh.devices.reshape(mesh.shape["pb"], 2, 8, 2), ("pb", "ka_0", "ka_1", "ka_2"))
    placed = (P(KA, "pb"), P("pb", None), P("pb", KA), P("pb", None))
    return jax.shard_map(
        per_device, mesh=split, in_specs=placed, out_specs=P("pb", KA), check_vma=False
    )
```

profile of v0, /device:TPU:1, one launch (start us, length us, event | category | flops | bytes accessed | tf_op | source)
XLA Modules:
  0.0 211.1 jit_solution(11353206829914429534)
XLA Ops:
  6.5 1.1 copy-done
  7.6 1.3 fusion.39
  8.9 26.7 %all_to_all.10 = f32[16,16,576]{2,1,0:T(8,128)S(1)} all-to-all(f32[16,16,576]{2,1,0:T(8,128)S(1)} %bitcast.112), channel_id=1, replica_groups=mesh['pb'=16,'ka_0'=2,'ka_1'=8,'ka_2'=2] {'pb'}, dimensions={0} | all-to-all | bytes 1179648 | tf_op jit(solution)/shard_map/all_to_all | solution.py:24
  35.6 0.9 broadcast_in_dim.36
  36.5 3.6 %all-to-all-start.1 = ((f32[16,16,576]{2,1,0:T(8,128)}), f32[16,16,576]{2,1,0:T(8,128)S(1)}, u32[]{:S(2)}, u32[]{:S(2)}) async-start(f32[16,16,576]{2,1,0:T(8,128)} %broadcast_in_dim.36), calls=%async_computation.1 | async-start | bytes 1310720 | tf_op jit(solution)/shard_map/all_to_all | solution.py:41
  40.2 0.1 fusion.34
  40.3 0.1 reshape.215
  40.4 0.2 reduce_window_sum.11
  40.6 0.7 fusion.36
  43.4 15.3 %all-to-all-done.1 = f32[16,16,576]{2,1,0:T(8,128)S(1)} async-done(((f32[16,16,576]{2,1,0:T(8,128)}), f32[16,16,576]{2,1,0:T(8,128)S(1)}, u32[]{:S(2)}, u32[]{:S(2)}) %all-to-all-start.1) | async-done | bytes 589856 | tf_op jit(solution)/shard_map/all_to_all | solution.py:41
  58.6 0.1 fusion.38
  58.7 0.1 multiply_reduce_fusion
  59.0 0.2 fusion.33
  59.2 0.1 copy.92
  59.4 0.1 copy.93
  59.5 0.1 multiply_convert_fusion
  59.6 0.1 fusion.25
  59.7 0.1 copy.83
  59.8 13.1 %all_gather.9 = bf16[2,128,576]{1,2,0:T(8,128)(2,1)} all-gather(bf16[1,128,576]{1,2,0:T(8,128)(2,1)S(1)} %copy.83), channel_id=1, replica_groups=mesh['pb'=16,'ka_0'=2,'ka_1'=8,'ka_2'=2] {'ka_0'}, dimensions={0}, use_global_device_ids=true | all-gather | bytes 442368 | tf_op jit(solution)/shard_map/all_gather | solution.py:58
  73.0 40.8 %all-gather.3.cloned.1.call-done = bf16[16,128,576]{1,2,0:T(8,128)(2,1)} async-done(((bf16[2,128,576]{1,2,0:T(8,128)(2,1)}), bf16[16,128,576]{1,2,0:T(8,128)(2,1)}) %all-gather.3.cloned.1.call-update) | async-done | bytes 2359312 | tf_op jit(solution)/shard_map/all_gather | solution.py:58
  113.8 0.1 sub.25
  113.9 2.2 %reshape.233 = bf16[2,2,128,2,576]{4,3,2,1,0:T(2,128)(2,1)} reshape(bf16[512,1152]{1,0:T(8,128)(2,1)S(1)} %copy-done.2) | data formatting | bytes 2359296 | tf_op jit(solution)/shard_map/reshape | solution.py:125
  116.1 3.5 %copy.87 = bf16[2,2,128,2,576]{2,4,3,1,0:T(8,128)(2,1)S(1)} copy(bf16[2,2,128,2,576]{4,3,2,1,0:T(2,128)(2,1)} %reshape.233) | data formatting | bytes 2359296
  119.6 0.2 select_reduce_fusion
  119.8 22.4 %all-gather.5.cloned.1.call-done = bf16[32,128,576]{1,2,0:T(8,128)(2,1)} async-done(((bf16[16,128,576]{1,2,0:T(8,128)(2,1)}), bf16[32,128,576]{1,2,0:T(8,128)(2,1)}) %all-gather.5.cloned.1.call-update) | async-done | bytes 4718608 | tf_op jit(solution)/shard_map/all_gather | solution.py:58
  142.2 4.9 %copy.84 = bf16[2,8,2,128,576]{3,4,2,1,0:T(8,128)(2,1)} copy(bf16[2,8,2,128,576]{3,4,0,1,2:T(8,128)(2,1)} %bitcast.111) | data formatting | bytes 9437184 | tf_op jit(solution)/shard_map/transpose | solution.py:62
  147.1 7.6 %copy.86 = bf16[32,128,576]{2,1,0:T(8,128)(2,1)} copy(bf16[32,128,576]{1,2,0:T(8,128)(2,1)} %bitcast.107) | data formatting | bytes 9437184
  154.8 49.5 %while.13 = (s32[]{:T(128)}, bf16[2,256,1024]{2,1,0:T(8,128)(2,1)}, s32[2,2,16]{2,1,0:T(2,128)S(1)}, bf16[32,128,576]{2,1,0:T(8,128)(2,1)}, s32[2,2,16]{2,1,0:T(...) while((s32[]{:T(128)}, bf16[2,256,1024]{2,1,0:T(8,128)(2,1)}, ...), condition=%wide.region_9.10_spmd.clone.clone, body=%wide.region_6.9_spmd.clone.clone.sunk | while | flops 2292459520 | bytes 53653520 | solution.py:159
  154.8 0.6 dynamic_slice.73
  156.3 1.4 compare_and_fusion.2
  157.9 6.0 %gather_fusion = bf16[32,128,576]{2,1,0:T(8,128)(2,1)} fusion(bf16[32,128,576]{2,1,0:T(8,128)(2,1)} %get-tuple-element.272, s32[1024]{0:T(1024)S(1)} %pad_clamp_fusion.2), kind=kCustom, calls=%fused_computation.clone.clone.1 | custom fusion | bytes 9437312 | tf_op jit(solution)/shard_map/while/body/eval_jaxpr/gather | solution.py:129
  163.9 4.3 %fusion.51 = f32[2,2048,128,2]{2,1,3,0:T(8,128)S(1)} fusion(bf16[2,2048,576,1]{2,1,3,0:T(8,128)(2,1)} %bitcast.105, bf16[2,2,128,2,576]{2,4,3,1,0:T(8,128)(2,1)S(1)} %get-tuple-element.277, s32[]{:T(128)} %get-tuple-element.258), kind=kOutput, calls=%fused_computation.16.clone.1 | convolution fusion | flops 1207959552 | bytes 9502724 | tf_op jit(solution)/shard_map/while/body/eval_jaxpr/wfer,wur->wefu/dot_general | solution.py:132
  168.2 2.1 copy-done.1
  170.3 1.5 fusion.53
  171.8 6.1 %fusion.54 = bf16[2,128,2,512]{1,3,2,0:T(8,128)(2,1)S(1)} fusion(f32[2,2,128]{2,1,0:T(2,128)S(1)} %fusion.53, bf16[2,2048,576]{2,1,0:T(8,128)(2,1)} %bitcast.106, f32[2,2048,128,2]{2,1,3,0:T(8,128)} %copy-done.1, pred[2,128,2048]{1,2,0:T(8,128)(4,1)S(1)} %compare_and_fusion.2), kind=kOutput, calls=%fused_computation.15.clone.1 | convolution fusion | flops 1079249408 | bytes 9439232 | tf_op jit(solution)/shard_map/while/body/eval_jaxpr/stvl,slz->svtz/dot_general | solution.py:151
  177.9 0.5 copy.114
  178.3 0.4 broadcast_in_dim.117
  178.7 0.8 constant_dynamic-update-slice_fusion.2
  179.5 0.6 dynamic_slice.73
  181.1 1.4 compare_and_fusion.2
  182.6 6.0 %gather_fusion = bf16[32,128,576]{2,1,0:T(8,128)(2,1)} fusion(bf16[32,128,576]{2,1,0:T(8,128)(2,1)} %get-tuple-element.272, s32[1024]{0:T(1024)S(1)} %pad_clamp_fusion.2), kind=kCustom, calls=%fused_computation.clone.clone.1 | custom fusion | bytes 9437312 | tf_op jit(solution)/shard_map/while/body/eval_jaxpr/gather | solution.py:129
  188.7 4.3 %fusion.51 = f32[2,2048,128,2]{2,1,3,0:T(8,128)S(1)} fusion(bf16[2,2048,576,1]{2,1,3,0:T(8,128)(2,1)} %bitcast.105, bf16[2,2,128,2,576]{2,4,3,1,0:T(8,128)(2,1)S(1)} %get-tuple-element.277, s32[]{:T(128)} %get-tuple-element.258), kind=kOutput, calls=%fused_computation.16.clone.1 | convolution fusion | flops 1207959552 | bytes 9502724 | tf_op jit(solution)/shard_map/while/body/eval_jaxpr/wfer,wur->wefu/dot_general | solution.py:132
  193.0 2.1 copy-done.1
  195.0 1.5 fusion.53
  196.5 6.1 %fusion.54 = bf16[2,128,2,512]{1,3,2,0:T(8,128)(2,1)S(1)} fusion(f32[2,2,128]{2,1,0:T(2,128)S(1)} %fusion.53, bf16[2,2048,576]{2,1,0:T(8,128)(2,1)} %bitcast.106, f32[2,2048,128,2]{2,1,3,0:T(8,128)} %copy-done.1, pred[2,128,2048]{1,2,0:T(8,128)(4,1)S(1)} %compare_and_fusion.2), kind=kOutput, calls=%fused_computation.15.clone.1 | convolution fusion | flops 1079249408 | bytes 9439232 | tf_op jit(solution)/shard_map/while/body/eval_jaxpr/stvl,slz->svtz/dot_general | solution.py:151
  202.6 0.5 copy.114
  203.1 0.4 broadcast_in_dim.117
  203.4 0.8 constant_dynamic-update-slice_fusion.2
  (47 shorter events, 1.1 us)
Async XLA Ops:
  6.5 1.1 copy-start
  6.5 33.6 %copy-start.3 = (s32[4,16]{1,0:T(4,128)S(1)}, s32[4,16]{1,0:T(4,128)}, u32[]{:S(2)}) copy-start(s32[4,16]{1,0:T(4,128)} %param.9) | copy-start | bytes 772
  35.6 78.3 %copy-start.2 = (bf16[512,1152]{1,0:T(8,128)(2,1)S(1)}, bf16[512,1152]{1,0:T(8,128)(2,1)}, u32[]{:S(2)}) copy-start(bf16[512,1152]{1,0:T(8,128)(2,1)} %param.8) | copy-start | bytes 3538948
  36.5 22.1 %all-to-all-start.1 = ((f32[16,16,576]{2,1,0:T(8,128)}), f32[16,16,576]{2,1,0:T(8,128)S(1)}, u32[]{:S(2)}, u32[]{:S(2)}) async-start(f32[16,16,576]{2,1,0:T(8,128)} %broadcast_in_dim.36), calls=%async_computation.1 | async-start | bytes 1310720 | tf_op jit(solution)/shard_map/all_to_all | solution.py:41
  40.1 73.7 %all-gather.3.cloned.1.call-start = ((), (), s32[]{:S(2)}) async-start(), calls=%async_computation.2 | async-start | bytes 2654208 | tf_op jit(solution)/shard_map/all_gather | solution.py:58
  73.0 69.3 %all-gather.5.cloned.1.call-start = ((), (), s32[]{:S(2)}) async-start(), calls=%async_computation.3 | async-start | bytes 7077888 | tf_op jit(solution)/shard_map/all_gather | solution.py:58
  168.2 2.1 copy-start.1
  192.9 2.1 copy-start.1
Sparse Core Ops, SparseCore 0:
  73.1 40.6 all-gather.2
  115.9 26.3 all-gather.4
where the time goes:
time: 212 us; the launch traced here: 211 us
  waiting for transfers between devices  78.5 us (37%)
  local copies, waits for them, and re-layouts  42.1 us (20%)
  blocking collectives  39.7 us (19%)
  matrix products  22.1 us (10%)
  between operations  15.6 us (7%)
  other arithmetic  7.88 us (4%)
  starting transfers between devices  3.68 us (2%)
    all_gather x2, waiting for transfers between devices, gather_in_order(): pieces = lax.all_gather(pieces, axes[k], axis=0, tiled=True)  63.2 us
    all_to_all x1, blocking collectives, sum_at_owner(): lax.all_to_all(pieces, axis, split_axis=0, concat_axis=0, tiled=True)  26.7 us
    all_to_all x1, waiting for transfers between devices, from_everyone(): lax.all_to_all(jnp.broadcast_to(x[None], (devices, *x.shape)), axis, 0, 0...  15.3 us
    all_gather x1, blocking collectives, gather_in_order(): pieces = lax.all_gather(pieces, axes[k], axis=0, tiled=True)  13.1 us
    unnamed x10, local copies, waits for them, and re-layouts  12.3 us
    dot_general x2, matrix products, attend(): jnp.einsum('stvl,slz->svtz', weight_brain_float, selected_values, preferr...  12.2 us
    gather x2, local copies, waits for them, and re-layouts, attend(): selected_keys = pool_blocks[index_pair].reshape(2, MAXSEL * BLK, width)  12 us
    dot_general x2, matrix products, attend(): jnp.einsum('wfer,wur->wefu', query_couple, selected_keys, preferred_eleme...  8.56 us
  transfers between devices with their start and end apart: 3, of which 3 were waited for; matrix products, arithmetic and copies ran while one was open for 3% of the time, Pallas kernels for 0%

commit v1 on v0

v1 whole, which is shorter than its diff:
```python
import functools
import math

import jax
import jax.numpy as jnp
from jax import lax
from jax.experimental import pallas as pl
from jax.experimental.pallas import tpu as pltpu
from jax.sharding import PartitionSpec as P

KVL = 512
RD = 64
WIDTH = KVL + RD
QK = 192
BLK = 128
QB = 4
HEADS = 2
YL = 4
NEG = -1e30
FAR = 1 << 20
F32 = jnp.float32
BF16 = jnp.bfloat16
I16 = jnp.int16
TOP = 32000.0


def div(a, n):
    return lax.div(a, jnp.int32(n))


def rem(a, n):
    return lax.rem(a, jnp.int32(n))


def kernel(
    n_pb, n_z,
    tok_hbm, w_hbm, bl_hbm, q_hbm,
    out_ref,
    tok_ref, w_ref, bl_ref, qv,
    lat_pool, rot_pool, guest_lat, guest_rot, rs_send, rs_recv, rx_send, rx_recv, ag_send, pieces, qs, acc, m_scr, l_scr, p_scr, f_scr, lim_scr,
    in_sem, rs_ss, rs_rs, rx_ss, rx_rs, ag_ss, ag_rs, start_ss, ring_ss, core_ss, pool_rs,
    far_in, gring_rs, gstart_ss, gring_ss, gout_ss,
):
    pb = lax.axis_index("pb")
    ka = lax.axis_index("ka")
    n_ka = 4 * n_z
    piece = BLK // n_pb
    events = 2 * n_z
    last_turn = n_z // 2 - 1
    y = div(ka, 2 * n_z)
    z = rem(div(ka, 2), n_z)
    c = rem(ka, 2)
    far = rem(ka + 2 * n_z, n_ka)
    twin = ka + 1 - 2 * c
    shift = n_pb - YL
    heavy = div(pb, shift)
    flip = y * (1 - heavy)
    own_pair = div(ka, 2)
    far_pair = div(far, 2)

    def beside(step):
        return y * 2 * n_z + rem(z + step + n_z, n_z) * 2 + c

    def send(src, dst, send_sem, recv_sem, to):
        return pltpu.make_async_remote_copy(
            src_ref=src, dst_ref=dst, send_sem=send_sem, recv_sem=recv_sem,
            device_id=to, device_id_type=pl.DeviceIdType.MESH,
        )

    barrier = pltpu.get_barrier_semaphore()

    def greet(to):
        pl.semaphore_signal(barrier, inc=1, device_id=to, device_id_type=pl.DeviceIdType.MESH)

    def greet_row(d, _):
        greet((rem(pb + d, n_pb), ka))
        return 0

    loads = [
        pltpu.make_async_copy(src, dst, in_sem.at[n])
        for n, (src, dst) in enumerate(
            [(tok_hbm, tok_ref), (w_hbm, w_ref), (bl_hbm, bl_ref), (q_hbm, qv)]
        )
    ]
    for load in loads:
        load.start()
    lax.fori_loop(1, n_pb, greet_row, 0)
    greet((pb, far))
    greet((pb, beside(1)))
    greet((pb, beside(-1)))
    greet((pb, twin))

    for load in loads[:3]:
        load.wait()
    part = lax.dot_general(
        tok_ref[...], w_ref[...], (((0,), (0,)), ((), ())), preferred_element_type=F32
    )
    listed = bl_ref[...]
    picks = jnp.where(listed == 2 * ka + 1, 1.0, 0.0)
    picked = jnp.max(jnp.max(picks, axis=1, keepdims=True), axis=0, keepdims=True)
    flag = jnp.broadcast_to(picked, (piece, 128))
    latents = part[:, :KVL]
    peak = jnp.maximum(jnp.max(jnp.abs(latents), axis=1, keepdims=True), 1e-30)
    coded = jnp.round(latents * (TOP / peak))
    unit = peak * (1.0 / TOP)
    for j in range(n_pb):
        low, high = [part[b * BLK + piece * j : b * BLK + piece * (j + 1)] for b in range(2)]
        both = [coded[b * BLK + piece * j : b * BLK + piece * (j + 1)] for b in range(2)]
        rs_send[j] = jnp.concatenate(both, axis=0).astype(jnp.int32).astype(I16)
        units = [unit[b * BLK + piece * j : b * BLK + piece * (j + 1)] for b in range(2)]
        units = jnp.concatenate([jnp.broadcast_to(u, (piece, RD)) for u in units], axis=1)
        tail = jnp.concatenate([low[:, KVL:], high[:, KVL:]], axis=1)
        rx_send[j] = jnp.concatenate([tail, jnp.where(flag > 0.5, -units, units)], axis=0)

    pl.semaphore_wait(barrier, n_pb + 3)
    pl.semaphore_signal(
        far_in, inc=1, device_id=(pb, far), device_id_type=pl.DeviceIdType.MESH
    )

    def rs_copy(to, slot):
        return send(rs_send.at[to], rs_recv.at[slot], rs_ss.at[to], rs_rs.at[slot], (to, ka))

    def rx_copy(to, slot):
        return send(rx_send.at[to], rx_recv.at[slot], rx_ss.at[to], rx_rs.at[slot], (to, ka))

    def start_rs(d, _):
        to = rem(pb + d, n_pb)
        rs_copy(to, pb).start()
        rx_copy(to, pb).start()
        return 0

    lax.fori_loop(1, n_pb, start_rs, 0)

    loads[3].wait()
    for i in range(QB):
        rows = slice(i * BLK, (i + 1) * BLK)
        for h in range(HEADS):
            mine = slice(h * BLK, (h + 1) * BLK)
            near = qv[rows, h * KVL : h * KVL + KVL + 128].astype(F32)[:, h * RD : h * RD + WIDTH]
            none = jnp.zeros((BLK, RD), F32)
            turn = near[:, KVL:]
            qs[i, mine, :KVL] = near[:, :KVL].astype(BF16)
            qs[i, mine, KVL:] = jnp.concatenate([turn, none, none, turn], axis=1).astype(BF16)
    m_scr[...] = jnp.full_like(m_scr, NEG)
    l_scr[...] = jnp.zeros_like(l_scr)
    acc[...] = jnp.zeros_like(acc)
    p_scr[...] = jnp.zeros_like(p_scr)
    f_scr[...] = jnp.ones_like(f_scr)

    def reach(slot, _):
        first = jnp.max(jnp.where(listed == 2 * slot, 1.0, 0.0), axis=1, keepdims=True)
        other = jnp.max(jnp.where(listed == 2 * slot + 1, 1.0, 0.0), axis=1, keepdims=True)
        block = QB * pb + lax.broadcasted_iota(jnp.int32, (QB, 1), 0)
        gap = (block - 2 * slot) * BLK
        limit = jnp.where(first > 0.5, gap, jnp.where(other > 0.5, gap - BLK, -FAR))
        lim_scr[slot] = jnp.broadcast_to(limit, (QB, HEADS * BLK))
        return 0

    lax.fori_loop(0, n_ka, reach, 0)

    row = lax.broadcasted_iota(jnp.int32, (2 * piece, RD), 0)
    col = lax.broadcasted_iota(jnp.int32, (2 * piece, RD), 1)
    place = ka * 2 * BLK + (row // piece) * BLK + pb * piece + row % piece
    freq = jnp.exp((col % (RD // 2)).astype(F32) * (-2.0 * math.log(10000.0) / RD))
    angle = place.astype(F32) * freq
    cosine = jnp.cos(angle)
    sine = jnp.where(col < RD // 2, -jnp.sin(angle), jnp.sin(angle))

    def take_rs(d, total):
        q = rem(pb + d, n_pb)
        rs_copy(q, q).wait_recv()
        rx_copy(q, q).wait_recv()
        return total[0] + decoded(rs_recv[q], rx_recv[q]), total[1] + rx_recv[q]

    def decoded(codes, extra):
        units = jnp.abs(extra[piece:])
        units = jnp.concatenate([units[:, :1], units[:, RD : RD + 1]], axis=0)
        return codes.astype(jnp.int32).astype(F32) * units

    rx_recv[pb] = rx_send[pb]
    start = (decoded(rs_send[pb], rx_send[pb]), rx_send[pb])
    latent, tail = lax.fori_loop(1, n_pb, take_rs, start)
    latent = latent * lax.rsqrt(jnp.mean(latent * latent, axis=-1, keepdims=True) + 1e-06)
    tail = tail[:piece]
    rotary = jnp.concatenate([tail[:, :RD], tail[:, RD:]], axis=0)
    turned = jnp.concatenate([rotary[:, RD // 2 :], rotary[:, : RD // 2]], axis=1)
    rotary = rotary * cosine + turned * sine
    keys = jnp.concatenate([latent, rotary], axis=1)

    for p in range(n_pb):
        second = rx_recv[p][piece : piece + 1, :1] < 0.0
        ag_send[p] = jnp.where(second, keys[piece:], keys[:piece]).astype(BF16)
    pieces[0, pb] = ag_send[pb]
    lends = (y == 1) & (c == 1)

    @pl.when(lends & (pb < YL))
    def _():
        pieces[2, pb] = ag_send[pb + shift]

    def piece_copy(part, slot, send_sem, src, to):
        return send(ag_send.at[src], pieces.at[part, slot], send_sem, ag_rs.at[part, slot], to)

    def each_ag(f, to, act):
        lent = jnp.where(lends & (to >= shift), 1, 0)
        dest = to - lent * shift
        part = f + lent * (2 - f)
        there = (dest, ka if f == 0 else far)
        away = (own_pair <= to) & (dest != pb) if f == 0 else own_pair <= to

        @pl.when(away)
        def _():
            act(piece_copy(part, pb, ag_ss.at[f, to], to, there))

    def take_piece(part, q):
        piece_copy(part, q, ag_ss.at[0, q], q, (q, ka)).wait_recv()

    def start_ag(f, d):
        each_ag(f, rem(pb + d, n_pb), lambda copy: copy.start())
        return 0

    lax.fori_loop(0, n_pb, lambda d, _: start_ag(0, d), 0)
    pl.semaphore_wait(far_in, 1)
    lax.fori_loop(0, n_pb, lambda d, _: start_ag(1, d), 0)

    class Both:
        def __init__(self, slot, sems, to, src=None, dst=None):
            src_refs, src_at = src or ((lat_pool, rot_pool), slot)
            dst_refs, arrived, dst_at = dst or ((lat_pool, rot_pool), pool_rs, slot)
            self.copies = [
                send(src_refs[n].at[src_at], dst_refs[n].at[dst_at], sems.at[n], arrived.at[n, dst_at], to)
                for n in range(2)
            ]

        def start(self):
            for copy in self.copies:
                copy.start()

        def wait_send(self):
            for copy in self.copies:
                copy.wait_send()

        def wait_recv(self):
            for copy in self.copies:
                copy.wait_recv()

    def core_copy(k, pair):
        return Both(2 * pair + c, core_ss.at[k], (pb, twin))

    def carried(pair):
        return (heavy == 1) & (c == 1) & (pair >= n_z)

    def own_opening(f, act):
        slot, pair = (ka, own_pair) if f == 0 else (far, far_pair)
        for side in range(2):
            act(Both(slot, start_ss.at[f, side], (pb, beside(1 - 2 * side))))
        act(core_copy(rem(f + heavy * y, 2), pair))

    def fill(refs, at, block):
        refs[0][at] = block[:, :KVL].astype(BF16)
        halves = [block[: BLK // 2, KVL:], block[BLK // 2 :, KVL:]]
        refs[1][at] = jnp.concatenate(halves, axis=1).astype(BF16)

    def open_ring(f):
        slot, pair = (ka, own_pair) if f == 0 else (far, far_pair)

        @pl.when((pair <= pb) & jnp.logical_not(carried(pair)))
        def _():
            def take(d, _):
                q = rem(pb + d, n_pb)
                take_piece(f, q)
                return 0

            lax.fori_loop(1 - f, n_pb, take, 0)
            fill((lat_pool, rot_pool), slot, pieces[f].astype(F32).reshape(BLK, WIDTH))
            own_opening(f, lambda copy: copy.start())

    open_ring(0)
    open_ring(1)

    guests = (guest_lat, guest_rot)
    host = (pb < YL) & (c == 1)

    def guest_start(side):
        to = (pb, beside(1 - 2 * side))
        return Both(z, gstart_ss.at[side], to, (guests, z), (guests, gring_rs, z))

    def guest_relay(at, side):
        to = (pb, beside(1 - 2 * side))
        return Both(at, gring_ss.at[at], to, (guests, at), (guests, gring_rs, at))

    def guest_out(at):
        slot = 2 * (n_z + at) + 1
        pools = (lat_pool, rot_pool)
        return Both(at, gout_ss.at[at], (pb + shift, ka), (guests, at), (pools, pool_rs, slot))

    def early_side(turn):
        return jnp.where(rem(z - 1 - turn + n_z, n_z) < rem(z + 1 + turn, n_z), 0, 1)

    def guest_event(e):
        turn = div(e, 2)
        final = div(e, n_z - 2)
        side = final + (1 - final) * rem(e, 2)
        at = rem(z - (1 + turn) * (1 - 2 * side) + n_z, n_z)
        onward = (turn < last_turn - 1) | ((turn == last_turn - 1) & (side == 1))
        return at, side, onward

    @pl.when(host)
    def _():
        @pl.when(n_z + z <= pb + shift)
        def _():
            def take(d, _):
                q = rem(pb + d, n_pb)

                @pl.when((d > 0) | (y == 0))
                def _():
                    take_piece(2, q)

                return 0

            lax.fori_loop(0, n_pb, take, 0)
            fill(guests, z, pieces[2].astype(F32).reshape(BLK, WIDTH))
            guest_start(0).start()
            guest_start(1).start()
            guest_out(z).start()

    def event(k):
        opening = 1 - div(k + events - 2, events)
        j = (k - 2) * (1 - opening)
        turn = div(j, 4)
        last = div(turn, last_turn)
        side = rem(j, 2)
        g = last * side + (1 - last) * rem(flip + div(j, 2), 2)
        at = rem(z - (1 + turn) * (1 - 2 * side) + n_z, n_z)
        pair = opening * (rem(flip + k, 2) * n_z + z) + (1 - opening) * (g * n_z + at)
        onward = (turn < last_turn - 1) | ((turn == last_turn - 1) & (g == side))
        lent = carried(pair)
        live = (pair <= pb) & ((k >= 2) | lent)
        return pair, side, onward & jnp.logical_not(lent), live

    def relay_copy(k, pair, side):
        return Both(2 * pair + c, ring_ss.at[k], (pb, beside(1 - 2 * side)))

    scale = math.log2(math.e) / math.sqrt(QK)
    shape = (BLK, HEADS * BLK)
    ahead = (
        lax.broadcasted_iota(jnp.int32, shape, 0) - lax.broadcasted_iota(jnp.int32, shape, 1) % BLK
    )

    def blend(i, values):
        return acc[i] * f_scr[i] + jnp.dot(values, p_scr[i], preferred_element_type=F32)

    def values_of(pair):
        return lat_pool[pl.ds(2 * pair, 2)].reshape(2 * BLK, KVL).T

    def attend(pair, before_pair):
        latents = lat_pool[pl.ds(2 * pair, 2)].reshape(2 * BLK, KVL)
        values = values_of(before_pair)
        none = jnp.zeros((BLK // 2, 128), BF16)
        parts = []
        for n in range(2):
            turn = rot_pool[2 * pair + n]
            parts += [jnp.concatenate([turn, none], 1), jnp.concatenate([none, turn], 1)]
        both = jnp.concatenate([latents, jnp.concatenate(parts, axis=0)], axis=1)
        limits = [lim_scr[2 * pair], lim_scr[2 * pair + 1]]

        def score(i):
            return lax.dot_general(
                both, qs[i], (((1,), (1,)), ((), ())), preferred_element_type=F32
            )

        scores = score(0)
        for i in range(QB):
            following = score(i + 1) if i + 1 < QB else None
            acc[i] = blend(i, values)
            seen = [
                jnp.where(ahead <= limits[n][i : i + 1], scores[n * BLK : (n + 1) * BLK], NEG)
                for n in range(2)
            ]
            scores = jnp.concatenate(seen, axis=0)
            before = m_scr[i]
            highest = jnp.maximum(before, jnp.max(scores, axis=0, keepdims=True))
            weights = jnp.exp2((scores - highest) * scale)
            fade = jnp.exp2((before - highest) * scale)
            l_scr[i] = l_scr[i] * fade + jnp.sum(weights, axis=0, keepdims=True)
            m_scr[i] = highest
            p_scr[i] = weights.astype(BF16)
            f_scr[i] = fade
            scores = following

    def drain_ring(k, _):
        pair, side, onward, live = event(k)

        @pl.when(live)
        def _():
            @pl.when(onward & (k >= 2))
            def _():
                relay_copy(k, pair, side).wait_send()

            core_copy(k, pair).wait_send()

        return 0

    def step(k, state):
        earlier, attended = state
        pair, side, onward, live = event(rem(k, events))

        @pl.when((k < events) & (k != events - 2) & live)
        def _():
            slot = 2 * pair + c
            Both(slot, core_ss.at[0], (pb, twin)).wait_recv()

            @pl.when(onward & (k >= 2))
            def _():
                relay_copy(k, pair, side).start()

            core_copy(k, pair).start()

        @pl.when(host & (k >= 1) & (k < n_z))
        def _():
            at, side, onward = guest_event(k - 1)

            @pl.when(n_z + at <= pb + shift)
            def _():
                guest_relay(at, side).wait_recv()

                @pl.when(onward)
                def _():
                    guest_relay(at, side).start()

                guest_out(at).start()


        ready = (k >= 1) & (earlier <= pb)

        @pl.when(ready)
        def _():
            Both(2 * earlier + 1 - c, core_ss.at[0], (pb, twin)).wait_recv()
            attend(earlier, jnp.where(attended < 0, earlier, attended))

        @pl.when(k == events - 2)
        def _():
            lax.fori_loop(0, events - 4, drain_ring, 0)

        @pl.when((k == events - 2) & live)
        def _():
            Both(2 * pair + c, core_ss.at[0], (pb, twin)).wait_recv()
            core_copy(k, pair).start()

        return pair, jnp.where(ready, earlier, attended)

    def drain_row(d, _):
        to = rem(pb + d, n_pb)

        @pl.when(d > 0)
        def _():
            rs_copy(to, pb).wait_send()
            rx_copy(to, pb).wait_send()

        each_ag(0, to, lambda copy: copy.wait_send())
        each_ag(1, to, lambda copy: copy.wait_send())
        return 0

    lax.fori_loop(0, n_pb, drain_row, 0)
    for f in range(2):
        pair = own_pair if f == 0 else far_pair

        @pl.when((pair <= pb) & jnp.logical_not(carried(pair)))
        def _():
            own_opening(f, lambda copy: copy.wait_send())

    _, attended = lax.fori_loop(0, events + 1, step, (jnp.int32(0), jnp.int32(-1)))

    values = values_of(attended)
    for i in range(QB):
        found = (blend(i, values) / l_scr[i]).astype(BF16)
        for h in range(HEADS):
            out_ref[i * BLK : (i + 1) * BLK, h * KVL : (h + 1) * KVL] = found[
                :, h * BLK : (h + 1) * BLK
            ].T

    lax.fori_loop(events - 4, events, drain_ring, 0)

    @pl.when(host)
    def _():
        @pl.when(n_z + z <= pb + shift)
        def _():
            guest_start(0).wait_send()
            guest_start(1).wait_send()
            guest_out(z).wait_send()

        def finish(e, _):
            at, side, onward = guest_event(e)

            @pl.when(n_z + at <= pb + shift)
            def _():
                @pl.when(onward)
                def _():
                    guest_relay(at, side).wait_send()

                guest_out(at).wait_send()

            return 0

        lax.fori_loop(0, n_z - 1, finish, 0)


def per_device(n_pb, n_z, tokens, kv_weight, queries, block_list):
    n_ka = 4 * n_z
    piece = BLK // n_pb
    rows = QB * BLK
    hbm = pl.BlockSpec(memory_space=pltpu.HBM)
    dma = pltpu.SemaphoreType.DMA
    return pl.pallas_call(
        functools.partial(kernel, n_pb, n_z),
        out_shape=jax.ShapeDtypeStruct((rows, HEADS * KVL), BF16),
        in_specs=[hbm, hbm, hbm, hbm],
        out_specs=pl.BlockSpec(memory_space=pltpu.VMEM),
        scratch_shapes=[
            pltpu.VMEM(tokens.shape[::-1], BF16),
            pltpu.VMEM(kv_weight.shape, BF16),
            pltpu.VMEM(block_list.shape, jnp.int32),
            pltpu.VMEM(queries.shape, BF16),
            pltpu.VMEM((n_ka, BLK, KVL), BF16),
            pltpu.VMEM((n_ka, BLK // 2, 2 * RD), BF16),
            pltpu.VMEM((n_z, BLK, KVL), BF16),
            pltpu.VMEM((n_z, BLK // 2, 2 * RD), BF16),
            pltpu.VMEM((n_pb, 2 * piece, KVL), I16),
            pltpu.VMEM((n_pb, 2 * piece, KVL), I16),
            pltpu.VMEM((n_pb, 2 * piece, 2 * RD), F32),
            pltpu.VMEM((n_pb, 2 * piece, 2 * RD), F32),
            pltpu.VMEM((n_pb, piece, WIDTH), BF16),
            pltpu.VMEM((3, n_pb, piece, WIDTH), BF16),
            pltpu.VMEM((QB, HEADS * BLK, KVL + 4 * RD), BF16),
            pltpu.VMEM((QB, KVL, HEADS * BLK), F32),
            pltpu.VMEM((QB, 1, HEADS * BLK), F32),
            pltpu.VMEM((QB, 1, HEADS * BLK), F32),
            pltpu.VMEM((QB, 2 * BLK, HEADS * BLK), BF16),
            pltpu.VMEM((QB, 1, HEADS * BLK), F32),
            pltpu.VMEM((n_ka, QB, HEADS * BLK), jnp.int32),
            dma((4,)),
            dma((n_pb,)),
            dma((n_pb,)),
            dma((n_pb,)),
            dma((n_pb,)),
            dma((2, n_pb)),
            dma((3, n_pb)),
            dma((2, 2, 2)),
            dma((2 * n_z, 2)),
            dma((2 * n_z, 2)),
            dma((2, n_ka)),
            pltpu.SemaphoreType.REGULAR,
            dma((2, n_z)),
            dma((2, 2)),
            dma((n_z, 2)),
            dma((n_z, 2)),
        ],
        compiler_params=pltpu.CompilerParams(
            collective_id=0, has_side_effects=True, vmem_limit_bytes=48 << 20
        ),
    )(*[pltpu.with_memory_space_constraint(a, pltpu.HBM) for a in (tokens.T, kv_weight, block_list, queries)])


def solution(mesh):
    n_pb, n_ka = mesh.shape["pb"], mesh.shape["ka"]
    return jax.shard_map(
        functools.partial(per_device, n_pb, n_ka // 4),
        mesh=mesh,
        in_specs=(P("ka", "pb"), P("pb", None), P("pb", "ka"), P("pb", None)),
        out_specs=P("pb", "ka"),
        check_vma=False,
    )
```

time: 212 us -> 63.2 us (0.30)
  the two profiles are of different devices: /device:TPU:1 before, /device:TPU:55 now
where the time goes in v1:
time: 63.2 us; the launch traced here: 63 us
  Pallas kernels  62.1 us (98%)
  local copies, waits for them, and re-layouts  0.97 us (2%)
    pallas_call x1, Pallas kernels, per_device(): pl.pallas_call(functools.partial(kernel, n_pb, n_z), out_shape=jax.ShapeD...  62.1 us

profile of v1, /device:TPU:55, one launch (start us, length us, event | category | flops | bytes accessed | tf_op | source)
XLA Modules:
  0.0 63.0 jit_solution(14148334498976674878)
XLA Ops:
  0.0 62.1 %shard_map.46 = bf16[512,1024]{1,0:T(8,128)(2,1)S(1)} custom-call(bf16[448,256]{1,0:T(8,128)(2,1)} %bitcast.1, bf16[448,576]{1,0:T(8,128)(2,1)} %w_hbm.1, s32[4,16]{1,0:T(4,128)} %bl_hbm.1, bf16[512,1152]{1,0:T(8,128)(2,1)} %q_hbm.1), custom_call_target="tpu_custom_call" | custom-call | tf_op jit(solution)/shard_map/pallas_call | solution.py:513
  62.1 1.0 %copy.6 = bf16[512,1024]{1,0:T(8,128)(2,1)} copy(bf16[512,1024]{1,0:T(8,128)(2,1)S(1)} %shard_map.46) | data formatting | bytes 2097152

commit v2 on v1

--- a/solution.py
+++ b/solution.py
@@ -20,8 +20,6 @@
 FAR = 1 << 20
 F32 = jnp.float32
 BF16 = jnp.bfloat16
-I16 = jnp.int16
-TOP = 32000.0
 
 
 def div(a, n):
@@ -99,18 +97,11 @@
     picks = jnp.where(listed == 2 * ka + 1, 1.0, 0.0)
     picked = jnp.max(jnp.max(picks, axis=1, keepdims=True), axis=0, keepdims=True)
     flag = jnp.broadcast_to(picked, (piece, 128))
-    latents = part[:, :KVL]
-    peak = jnp.maximum(jnp.max(jnp.abs(latents), axis=1, keepdims=True), 1e-30)
-    coded = jnp.round(latents * (TOP / peak))
-    unit = peak * (1.0 / TOP)
     for j in range(n_pb):
         low, high = [part[b * BLK + piece * j : b * BLK + piece * (j + 1)] for b in range(2)]
-        both = [coded[b * BLK + piece * j : b * BLK + piece * (j + 1)] for b in range(2)]
-        rs_send[j] = jnp.concatenate(both, axis=0).astype(jnp.int32).astype(I16)
-        units = [unit[b * BLK + piece * j : b * BLK + piece * (j + 1)] for b in range(2)]
-        units = jnp.concatenate([jnp.broadcast_to(u, (piece, RD)) for u in units], axis=1)
+        rs_send[j] = jnp.concatenate([low[:, :KVL], high[:, :KVL]], axis=0)
         tail = jnp.concatenate([low[:, KVL:], high[:, KVL:]], axis=1)
-        rx_send[j] = jnp.concatenate([tail, jnp.where(flag > 0.5, -units, units)], axis=0)
+        rx_send[j] = jnp.concatenate([tail, flag], axis=0)
 
     pl.semaphore_wait(barrier, n_pb + 3)
     pl.semaphore_signal(
@@ -170,15 +161,10 @@
         q = rem(pb + d, n_pb)
         rs_copy(q, q).wait_recv()
         rx_copy(q, q).wait_recv()
-        return total[0] + decoded(rs_recv[q], rx_recv[q]), total[1] + rx_recv[q]
-
-    def decoded(codes, extra):
-        units = jnp.abs(extra[piece:])
-        units = jnp.concatenate([units[:, :1], units[:, RD : RD + 1]], axis=0)
-        return codes.astype(jnp.int32).astype(F32) * units
+        return total[0] + rs_recv[q], total[1] + rx_recv[q]
 
     rx_recv[pb] = rx_send[pb]
-    start = (decoded(rs_send[pb], rx_send[pb]), rx_send[pb])
+    start = (rs_send[pb], rx_send[pb])
     latent, tail = lax.fori_loop(1, n_pb, take_rs, start)
     latent = latent * lax.rsqrt(jnp.mean(latent * latent, axis=-1, keepdims=True) + 1e-06)
     tail = tail[:piece]
@@ -188,7 +174,7 @@
     keys = jnp.concatenate([latent, rotary], axis=1)
 
     for p in range(n_pb):
-        second = rx_recv[p][piece : piece + 1, :1] < 0.0
+        second = rx_recv[p][piece : piece + 1, :1] > 0.5
         ag_send[p] = jnp.where(second, keys[piece:], keys[:piece]).astype(BF16)
     pieces[0, pb] = ag_send[pb]
     lends = (y == 1) & (c == 1)
@@ -524,8 +510,8 @@
             pltpu.VMEM((n_ka, BLK // 2, 2 * RD), BF16),
             pltpu.VMEM((n_z, BLK, KVL), BF16),
             pltpu.VMEM((n_z, BLK // 2, 2 * RD), BF16),
-            pltpu.VMEM((n_pb, 2 * piece, KVL), I16),
-            pltpu.VMEM((n_pb, 2 * piece, KVL), I16),
+            pltpu.VMEM((n_pb, 2 * piece, KVL), F32),
+            pltpu.VMEM((n_pb, 2 * piece, KVL), F32),
             pltpu.VMEM((n_pb, 2 * piece, 2 * RD), F32),
             pltpu.VMEM((n_pb, 2 * piece, 2 * RD), F32),
             pltpu.VMEM((n_pb, piece, WIDTH), BF16),

time: 63.2 us -> 66.6 us (1.054)
  Pallas kernels: 62.1 us -> 65.5 us
    pallas_call x1, Pallas kernels: 62.1 us -> 65.5 us  [per_device(): pl.pallas_call(functools.partial(kernel, n_pb, n_z), out_shape=jax.ShapeD...]
where the time goes in v2:
time: 66.6 us; the launch traced here: 66.5 us
  Pallas kernels  65.5 us (98%)
  local copies, waits for them, and re-layouts  0.97 us (1%)
    pallas_call x1, Pallas kernels, per_device(): pl.pallas_call(functools.partial(kernel, n_pb, n_z), out_shape=jax.ShapeD...  65.5 us

profile of v2, /device:TPU:55, one launch (start us, length us, event | category | flops | bytes accessed | tf_op | source)
XLA Modules:
  0.0 66.5 jit_solution(479220657265472511)
XLA Ops:
  0.0 65.5 %shard_map.46 = bf16[512,1024]{1,0:T(8,128)(2,1)S(1)} custom-call(bf16[448,256]{1,0:T(8,128)(2,1)} %bitcast.1, bf16[448,576]{1,0:T(8,128)(2,1)} %w_hbm.1, s32[4,16]{1,0:T(4,128)} %bl_hbm.1, bf16[512,1152]{1,0:T(8,128)(2,1)} %q_hbm.1), custom_call_target="tpu_custom_call" | custom-call | tf_op jit(solution)/shard_map/pallas_call | solution.py:499
  65.5 1.0 %copy.6 = bf16[512,1024]{1,0:T(8,128)(2,1)} copy(bf16[512,1024]{1,0:T(8,128)(2,1)S(1)} %shard_map.46) | data formatting | bytes 2097152
